TPU v7x, 32 devices: a whole 2x2x4 slice. The times are simulated.
32 devices in a mesh: dp: 8 (over z, x), tm: 4 (over y, core).
Axes of the slice: x: 2, y: 2, z: 4, core: 2. Of those that a mesh axis runs over, the one named last changes fastest.
Arguments:
- clips: bfloat16 [8, 32, 16, 16, 256], P('dp', 'tm'), may hold values from -6 to 6
- frame_counts: int32 [8], P('dp'), may hold values from 5 to 32, as said below
- weight: bfloat16 [6912, 256], P('dp'), may hold values from -0.078125 to 0.078125
- gain: float32 [256], replicated, may hold values from 0.1 to 1.9
- bias: float32 [256], replicated, may hold values from -3 to 3
- cotangent: bfloat16 [8, 16, 8, 8, 256], P('dp', 'tm'), may hold values from -6 to 6
Outputs:
- output: bfloat16 [8, 16, 8, 8, 256], P('dp', 'tm')
- input_grad: bfloat16 [8, 32, 16, 16, 256], P('dp', 'tm')
- weight_grad: float32 [6912, 256], P('dp')
Inputs may be any that keep to these rules, and one draw needn't show every extreme that they name: frame_counts[c] frames of clip c are valid, the remaining slots are padding; in every draw some clip uses all 32 slots.
All inputs are finite; a program needn't handle non-finite values.
Results may differ from a plain program's by a relative error of at most 0.0048.
Values may be sent and summed in bfloat16 or wider, within the bound.
A program may use at most 64 MiB of HBM per device.

v0:
```python
import jax
import jax.numpy as jnp
from jax import lax
from jax.sharding import PartitionSpec as P

GROUPS = 32
EPS = 1e-06


def shifted(value, axis, by):
    devices = lax.axis_size(axis)
    pairs = [(i, i + by) for i in range(devices) if 0 <= i + by < devices]
    return lax.ppermute(value, axis, pairs)


def unfold(padded, frames_out, rows_out, cols_out):
    tap_list = []
    for step_t in range(3):
        for step_r in range(3):
            for step_c in range(3):
                tap_piece = padded[
                    step_t : step_t + 2 * frames_out : 2,
                    step_r : step_r + 2 * rows_out : 2,
                    step_c : step_c + 2 * cols_out : 2,
                    :,
                ]
                tap_list.append(tap_piece.reshape(frames_out * rows_out * cols_out, -1))
    return jnp.concatenate(tap_list, axis=1)


def spread_taps(values, data_axis, tap_axis, length):
    moved = jnp.moveaxis(values, tap_axis, 0)
    count = moved.shape[data_axis + 1]
    width_list = [(0, 0)] * (moved.ndim - 1)
    after = list(width_list)
    after[data_axis] = (0, 1)
    before = list(width_list)
    before[data_axis] = (1, 0)
    even_part = jnp.pad(moved[0], after) + jnp.pad(moved[2], before)
    odd_part = jnp.pad(moved[1], after)
    joined = jnp.stack([even_part, odd_part], axis=data_axis + 1)
    shape_new = list(even_part.shape)
    shape_new[data_axis] = 2 * (count + 1)
    joined = joined.reshape(shape_new)
    return lax.slice_in_dim(joined, 0, length, axis=data_axis)


def fold_back(columns, padded_shape, frames_out, rows_out, cols_out):
    channels = padded_shape[3]
    blocks = columns.reshape(frames_out, rows_out, cols_out, 3, 3, 3, channels)
    blocks = spread_taps(blocks, 0, 3, padded_shape[0])
    blocks = spread_taps(blocks, 1, 3, padded_shape[1])
    blocks = spread_taps(blocks, 2, 3, padded_shape[2])
    return blocks


def silu_slope(preact):
    sig = jax.nn.sigmoid(preact)
    return sig * (1.0 + preact * (1.0 - sig))


def shards(clips, frame_counts, weight, gain, bias, cotangent):
    clip_data = clips[0]
    cot_block = cotangent[0]
    frame_count, row_count, col_count, channels = clip_data.shape
    width_g = channels // GROUPS
    first_frame = lax.axis_index("tm") * frame_count
    frame_mask = (first_frame + jnp.arange(frame_count) < frame_counts[0]).astype(jnp.float32)[
        :, None, None, None
    ]
    mask_group = frame_mask[..., None]
    entries = frame_counts[0].astype(jnp.float32) * (row_count * col_count * width_g)
    values = clip_data.astype(jnp.float32).reshape(
        frame_count, row_count, col_count, GROUPS, width_g
    )
    sum_first, sum_second = lax.psum(
        (
            jnp.sum(values * mask_group, axis=(0, 1, 2, 4)),
            jnp.sum(values * values * mask_group, axis=(0, 1, 2, 4)),
        ),
        "tm",
    )
    group_mean = sum_first / entries
    variance = sum_second / entries - group_mean * group_mean
    inv_std = lax.rsqrt(variance + EPS)
    normed_g = (values - group_mean[:, None]) * inv_std[:, None]
    normed = normed_g.reshape(frame_count, row_count, col_count, channels)
    preact = normed * gain + bias
    hidden = (jax.nn.silu(preact) * frame_mask).astype(jnp.bfloat16)
    earlier = shifted(hidden[-2:], "tm", 1)
    padded = jnp.pad(jnp.concatenate([earlier, hidden], axis=0), ((0, 0), (1, 0), (1, 0), (0, 0)))
    frames_out, rows_out, cols_out = (frame_count // 2, row_count // 2, col_count // 2)
    patches = unfold(padded, frames_out, rows_out, cols_out)
    cot_rows = cot_block.reshape(-1, channels)
    full_weight = lax.all_gather(weight, "dp", axis=0, tiled=True)
    out_rows = jnp.dot(patches, full_weight, preferred_element_type=jnp.float32)
    out_block = out_rows.astype(jnp.bfloat16).reshape(frames_out, rows_out, cols_out, channels)
    dcols = lax.dot_general(
        cot_rows, full_weight, (((1,), (1,)), ((), ())), preferred_element_type=jnp.float32
    )
    dpad = fold_back(dcols, padded.shape, frames_out, rows_out, cols_out)
    passed = shifted(dpad[:2, 1:, 1:, :], "tm", -1)
    dlocal = dpad[2:, 1:, 1:, :]
    dhidden = jnp.concatenate([dlocal[:-2], dlocal[-2:] + passed], axis=0)
    dnormed = dhidden * frame_mask * silu_slope(preact) * gain
    grad_norm = dnormed.reshape(frame_count, row_count, col_count, GROUPS, width_g)
    back_first, back_second = lax.psum(
        (jnp.sum(grad_norm, axis=(0, 1, 2, 4)), jnp.sum(grad_norm * normed_g, axis=(0, 1, 2, 4))),
        "tm",
    )
    input_grad = (
        mask_group
        * inv_std[:, None]
        * (grad_norm - back_first[:, None] / entries - normed_g * back_second[:, None] / entries)
    )
    input_grad = input_grad.reshape(frame_count, row_count, col_count, channels).astype(
        jnp.bfloat16
    )
    local_grad = lax.dot_general(
        patches, cot_rows, (((0,), (0,)), ((), ())), preferred_element_type=jnp.float32
    )
    clip_grad = lax.psum(local_grad, "tm")
    weight_grad = lax.psum_scatter(clip_grad, "dp", scatter_dimension=0, tiled=True)
    return (out_block[None], input_grad[None], weight_grad)


def solution(mesh):
    placed = (
        P("dp", "tm", None, None, None),
        P("dp"),
        P("dp", None),
        P(),
        P(),
        P("dp", "tm", None, None, None),
    )
    return jax.shard_map(
        shards,
        mesh=mesh,
        in_specs=placed,
        out_specs=(P("dp", "tm", None, None, None), P("dp", "tm", None, None, None), P("dp", None)),
        check_vma=False,
    )
```

profile of v0, /device:TPU:0, one launch (start us, length us, event | category | flops | bytes accessed | tf_op | source)
XLA Modules:
  0.0 398.6 jit_solution(1808083092063788715)
XLA Ops:
  8.6 1.8 fusion.18
  10.9 8.4 %all-reduce.11 = (f32[32]{0:T(128)S(1)}, f32[32]{0:T(128)S(1)}) all-reduce(f32[32]{0:T(128)S(1)} %reduce_sum.51, f32[32]{0:T(128)S(1)} %reduce_sum.54), channel_id=1, replica_groups=mesh['dp'=8,'tm'=4] {'tm'}, use_global_device_ids=true, to_apply=%region_2.0 | all-reduce | flops 64 | bytes 512 | tf_op jit(solution)/shard_map/psum | solution.py:76
  19.6 2.1 fusion.15
  34.1 9.8 %slice.146 = bf16[4,8,8,256]{3,2,1,0:T(8,128)(2,1)} slice(bf16[10,17,17,256]{3,2,1,0:T(8,128)(2,1)S(1)} %fusion.38), slice={[1:9:2], [2:17:2], [1:17:2], [0:256:1]} | slice | bytes 262144 | tf_op jit(solution)/shard_map/slice | solution.py:21
  43.9 9.7 %slice.145 = bf16[4,8,8,256]{3,2,1,0:T(8,128)(2,1)} slice(bf16[10,17,17,256]{3,2,1,0:T(8,128)(2,1)S(1)} %fusion.38), slice={[1:9:2], [2:17:2], [0:16:2], [0:256:1]} | slice | bytes 262144 | tf_op jit(solution)/shard_map/slice | solution.py:21
  53.6 9.8 %slice.144 = bf16[4,8,8,256]{3,2,1,0:T(8,128)(2,1)} slice(bf16[10,17,17,256]{3,2,1,0:T(8,128)(2,1)S(1)} %fusion.38), slice={[1:9:2], [1:17:2], [2:17:2], [0:256:1]} | slice | bytes 262144 | tf_op jit(solution)/shard_map/slice | solution.py:21
  63.4 9.7 %slice.143 = bf16[4,8,8,256]{3,2,1,0:T(8,128)(2,1)} slice(bf16[10,17,17,256]{3,2,1,0:T(8,128)(2,1)S(1)} %fusion.38), slice={[1:9:2], [1:17:2], [1:17:2], [0:256:1]} | slice | bytes 262144 | tf_op jit(solution)/shard_map/slice | solution.py:21
  73.1 9.7 %slice.142 = bf16[4,8,8,256]{3,2,1,0:T(8,128)(2,1)} slice(bf16[10,17,17,256]{3,2,1,0:T(8,128)(2,1)S(1)} %fusion.38), slice={[1:9:2], [1:17:2], [0:16:2], [0:256:1]} | slice | bytes 262144 | tf_op jit(solution)/shard_map/slice | solution.py:21
  82.8 9.7 %slice.141 = bf16[4,8,8,256]{3,2,1,0:T(8,128)(2,1)} slice(bf16[10,17,17,256]{3,2,1,0:T(8,128)(2,1)S(1)} %fusion.38), slice={[1:9:2], [0:16:2], [2:17:2], [0:256:1]} | slice | bytes 262144 | tf_op jit(solution)/shard_map/slice | solution.py:21
  92.5 9.7 %slice.140 = bf16[4,8,8,256]{3,2,1,0:T(8,128)(2,1)} slice(bf16[10,17,17,256]{3,2,1,0:T(8,128)(2,1)S(1)} %fusion.38), slice={[1:9:2], [0:16:2], [1:17:2], [0:256:1]} | slice | bytes 262144 | tf_op jit(solution)/shard_map/slice | solution.py:21
  102.2 9.7 %slice.139 = bf16[4,8,8,256]{3,2,1,0:T(8,128)(2,1)} slice(bf16[10,17,17,256]{3,2,1,0:T(8,128)(2,1)S(1)} %fusion.38), slice={[1:9:2], [0:16:2], [0:16:2], [0:256:1]} | slice | bytes 262144 | tf_op jit(solution)/shard_map/slice | solution.py:21
  111.9 9.8 %slice.138 = bf16[4,8,8,256]{3,2,1,0:T(8,128)(2,1)} slice(bf16[10,17,17,256]{3,2,1,0:T(8,128)(2,1)S(1)} %fusion.38), slice={[0:8:2], [2:17:2], [2:17:2], [0:256:1]} | slice | bytes 262144 | tf_op jit(solution)/shard_map/slice | solution.py:21
  121.7 9.7 %slice.137 = bf16[4,8,8,256]{3,2,1,0:T(8,128)(2,1)} slice(bf16[10,17,17,256]{3,2,1,0:T(8,128)(2,1)S(1)} %fusion.38), slice={[0:8:2], [2:17:2], [1:17:2], [0:256:1]} | slice | bytes 262144 | tf_op jit(solution)/shard_map/slice | solution.py:21
  131.4 9.7 %slice.136 = bf16[4,8,8,256]{3,2,1,0:T(8,128)(2,1)} slice(bf16[10,17,17,256]{3,2,1,0:T(8,128)(2,1)S(1)} %fusion.38), slice={[0:8:2], [2:17:2], [0:16:2], [0:256:1]} | slice | bytes 262144 | tf_op jit(solution)/shard_map/slice | solution.py:21
  141.1 9.8 %slice.135 = bf16[4,8,8,256]{3,2,1,0:T(8,128)(2,1)} slice(bf16[10,17,17,256]{3,2,1,0:T(8,128)(2,1)S(1)} %fusion.38), slice={[0:8:2], [1:17:2], [2:17:2], [0:256:1]} | slice | bytes 262144 | tf_op jit(solution)/shard_map/slice | solution.py:21
  150.9 9.7 %slice.134 = bf16[4,8,8,256]{3,2,1,0:T(8,128)(2,1)} slice(bf16[10,17,17,256]{3,2,1,0:T(8,128)(2,1)S(1)} %fusion.38), slice={[0:8:2], [1:17:2], [1:17:2], [0:256:1]} | slice | bytes 262144 | tf_op jit(solution)/shard_map/slice | solution.py:21
  160.6 9.7 %slice.133 = bf16[4,8,8,256]{3,2,1,0:T(8,128)(2,1)} slice(bf16[10,17,17,256]{3,2,1,0:T(8,128)(2,1)S(1)} %fusion.38), slice={[0:8:2], [1:17:2], [0:16:2], [0:256:1]} | slice | bytes 262144 | tf_op jit(solution)/shard_map/slice | solution.py:21
  170.3 9.8 %slice.132 = bf16[4,8,8,256]{3,2,1,0:T(8,128)(2,1)} slice(bf16[10,17,17,256]{3,2,1,0:T(8,128)(2,1)S(1)} %fusion.38), slice={[0:8:2], [0:16:2], [2:17:2], [0:256:1]} | slice | bytes 262144 | tf_op jit(solution)/shard_map/slice | solution.py:21
  180.1 9.7 %slice.131 = bf16[4,8,8,256]{3,2,1,0:T(8,128)(2,1)} slice(bf16[10,17,17,256]{3,2,1,0:T(8,128)(2,1)S(1)} %fusion.38), slice={[0:8:2], [0:16:2], [1:17:2], [0:256:1]} | slice | bytes 262144 | tf_op jit(solution)/shard_map/slice | solution.py:21
  189.8 9.7 %slice.130 = bf16[4,8,8,256]{3,2,1,0:T(8,128)(2,1)} slice(bf16[10,17,17,256]{3,2,1,0:T(8,128)(2,1)S(1)} %fusion.38), slice={[0:8:2], [0:16:2], [0:16:2], [0:256:1]} | slice | bytes 262144 | tf_op jit(solution)/shard_map/slice | solution.py:21
  212.5 1.7 copy-done.3
  214.3 4.1 %fusion.43 = f32[6912,256]{1,0:T(8,128)} fusion(bf16[256,6912]{1,0:T(8,128)(2,1)S(1)} %constant_dynamic-update-slice_fusion, bf16[256,256]{1,0:T(8,128)(2,1)S(1)} %bitcast.127), kind=kOutput, calls=%fused_computation.105 | convolution fusion | flops 905969664 | bytes 10747904 | tf_op jit(solution)/shard_map/dot_general | solution.py:119
  218.9 3.1 convolution_bitcast_fusion
  228.8 3.1 copy.39
  231.9 3.5 reshape.271
  238.2 1.9 slice_bitcast_fusion.7
  240.2 3.9 convolution_convert_fusion
  247.1 13.6 %all-reduce.10 = (f32[32]{0:T(128)S(1)}, f32[32]{0:T(128)S(1)}) all-reduce(f32[32]{0:T(128)S(1)} %reduce_sum.75, f32[32]{0:T(128)S(1)} %reduce_sum.72), channel_id=1, replica_groups=mesh['dp'=8,'tm'=4] {'tm'}, use_global_device_ids=true, to_apply=%region_11.12 | all-reduce | flops 64 | bytes 512 | tf_op jit(solution)/shard_map/psum | solution.py:107
  261.0 92.3 %reduce-scatter.2.cloned.1.call-done = f32[864,256]{1,0:T(8,128)} async-done(((f32[6912,256]{1,0:T(8,128)}), f32[864,256]{1,0:T(8,128)}) %reduce-scatter.2.cloned.1.call-update) | async-done | bytes 884752 | tf_op jit(solution)/shard_map/reduce_scatter | solution.py:123
  353.3 1.6 fusion.37
  354.9 35.1 %all-reduce.14.cloned.1.call-done = f32[864,256]{1,0:T(8,128)} async-done(((f32[864,256]{1,0:T(8,128)}), f32[864,256]{1,0:T(8,128)}) %all-reduce.14.cloned.1.call-update) | async-done | bytes 884752 | tf_op jit(solution)/shard_map/psum | solution.py:122
  390.0 2.1 copy.76
  (112 shorter events, 39.9 us)
Async XLA Ops:
  7.2 205.4 %copy-start = (bf16[1,4,8,8,256]{4,3,2,1,0:T(8,128)(2,1)S(1)}, bf16[1,4,8,8,256]{4,3,2,1,0:T(8,128)(2,1)}, u32[]{:S(2)}) copy-start(bf16[1,4,8,8,256]{4,3,2,1,0:T(8,128)(2,1)} %param.11) | copy-start | bytes 393220
  7.2 211.7 %all-gather.2.cloned.1.call-start = ((), (), s32[]{:S(2)}) async-start(), calls=%async_computation.1 | async-start | bytes 3981312 | tf_op jit(solution)/shard_map/all_gather | solution.py:95
  7.9 345.4 %reduce-scatter.2.cloned.1.call-start = ((), (), s32[]{:S(2)}) async-start(), calls=%async_computation.2 | async-start | bytes 7962624 | tf_op jit(solution)/shard_map/reduce_scatter | solution.py:123
  21.7 2.4 collective-permute-start
  201.1 11.1 %copy-start.9 = (bf16[4,8,8,256]{3,2,1,0:T(8,128)(2,1)S(1)}, bf16[4,8,8,256]{3,2,1,0:T(8,128)(2,1)}, u32[]{:S(2)}) copy-start(bf16[4,8,8,256]{3,2,1,0:T(8,128)(2,1)} %slice.142) | copy-start | bytes 393220
  201.1 11.2 %copy-start.8 = (bf16[4,8,8,256]{3,2,1,0:T(8,128)(2,1)S(1)}, bf16[4,8,8,256]{3,2,1,0:T(8,128)(2,1)}, u32[]{:S(2)}) copy-start(bf16[4,8,8,256]{3,2,1,0:T(8,128)(2,1)} %slice.143) | copy-start | bytes 393220
  201.1 11.2 %copy-start.7 = (bf16[4,8,8,256]{3,2,1,0:T(8,128)(2,1)S(1)}, bf16[4,8,8,256]{3,2,1,0:T(8,128)(2,1)}, u32[]{:S(2)}) copy-start(bf16[4,8,8,256]{3,2,1,0:T(8,128)(2,1)} %slice.144) | copy-start | bytes 393220
  201.1 11.2 %copy-start.6 = (bf16[4,8,8,256]{3,2,1,0:T(8,128)(2,1)S(1)}, bf16[4,8,8,256]{3,2,1,0:T(8,128)(2,1)}, u32[]{:S(2)}) copy-start(bf16[4,8,8,256]{3,2,1,0:T(8,128)(2,1)} %slice.145) | copy-start | bytes 393220
  201.1 11.2 %copy-start.5 = (bf16[4,8,8,256]{3,2,1,0:T(8,128)(2,1)S(1)}, bf16[4,8,8,256]{3,2,1,0:T(8,128)(2,1)}, u32[]{:S(2)}) copy-start(bf16[4,8,8,256]{3,2,1,0:T(8,128)(2,1)} %slice.146) | copy-start | bytes 393220
  212.5 1.8 copy-start.3
  218.4 171.6 %all-reduce.14.cloned.1.call-start = ((), (), s32[]{:S(2)}) async-start(), calls=%async_computation.3 | async-start | bytes 1769472 | tf_op jit(solution)/shard_map/psum | solution.py:122
  235.4 4.8 %copy-start.4 = (bf16[256,6912]{1,0:T(8,128)(2,1)S(1)}, bf16[256,6912]{1,0:T(8,128)(2,1)}, u32[]{:S(2)}) copy-start(bf16[256,6912]{1,0:T(8,128)(2,1)} %copy-done.3) | copy-start | bytes 10616836
  236.7 7.3 %collective-permute-start.1 = (f32[2,16,16,256]{3,2,1,0:T(8,128)S(1)}, f32[2,16,16,256]{3,2,1,0:T(8,128)S(1)}, u32[]{:S(2)}, u32[]{:S(2)}) collective-permute-start(f32[2,16,16,256]{3,2,1,0:T(8,128)S(1)} %slice.183), channel_id=1, source_target_pairs={{1,0},{2,1},{3,2},{5,4},{6,5},{7,6},{9,8},{10,9},{11,10},{13,12},{... | collective-permute-start | bytes 1572872 | tf_op jit(solution)/shard_map/ppermute | solution.py:13
  240.2 5.1 %copy-start.2 = (bf16[1,8,16,16,256]{4,3,2,1,0:T(8,128)(2,1)S(1)}, bf16[1,8,16,16,256]{4,3,2,1,0:T(8,128)(2,1)}, u32[]{:S(2)}) copy-start(bf16[1,8,16,16,256]{4,3,2,1,0:T(8,128)(2,1)} %param.6) | copy-start | bytes 3145732
  240.2 5.1 %copy-start.10 = (f32[256]{0:T(256)S(1)}, f32[256]{0:T(256)}, u32[]{:S(2)}) copy-start(f32[256]{0:T(256)} %param.10) | copy-start | bytes 3076
  240.2 5.1 %copy-start.11 = (f32[256]{0:T(256)S(1)}, f32[256]{0:T(256)}, u32[]{:S(2)}) copy-start(f32[256]{0:T(256)} %param.9) | copy-start | bytes 3076
  353.3 38.8 %copy-start.1 = (bf16[1,4,8,8,256]{4,3,2,1,0:T(8,128)(2,1)S(1)}, bf16[1,4,8,8,256]{4,3,2,1,0:T(8,128)(2,1)}, u32[]{:S(2)}) copy-start(bf16[1,4,8,8,256]{4,3,2,1,0:T(8,128)(2,1)} %param.11) | copy-start | bytes 393220
Sparse Core Ops, SparseCore 0:
  10.2 67.8 all-gather.1
  218.5 134.7 reduce-scatter.1
  355.8 34.1 all-reduce.13
where the time goes:
time: 399 us
  local copies, waits for them, and re-layouts  206 us (52%)
  waiting for transfers between devices  129 us (32%)
  blocking collectives  21.9 us (5%)
  between operations  15.1 us (4%)
  other arithmetic  12.5 us (3%)
  matrix products  11 us (3%)
    slice x27, local copies, waits for them, and re-layouts, unfold(): padded[step_t:step_t + 2 * frames_out:2, step_r:step_r + 2 * rows_out:2,...  176 us
    reduce_scatter x1, waiting for transfers between devices, shards(): lax.psum_scatter(clip_grad, 'dp', scatter_dimension=0, tiled=True)  92.3 us
    psum x1, waiting for transfers between devices, shards(): clip_grad = lax.psum(local_grad, 'tm')  35.1 us
    unnamed x51, local copies, waits for them, and re-layouts  15.1 us
    psum x1, blocking collectives, shards(): lax.psum((jnp.sum(grad_norm, axis=(0, 1, 2, 4)), jnp.sum(grad_norm * norm...  13.6 us
    psum x1, blocking collectives, shards(): lax.psum((jnp.sum(values * mask_group, axis=(0, 1, 2, 4)), jnp.sum(values...  8.37 us
  transfers between devices with their start and end apart: 5, of which 3 were waited for; matrix products, arithmetic and copies ran while one was open for 57% of the time, Pallas kernels for 0%

commit v1 on v0

--- a/solution.py
+++ b/solution.py
@@ -119,7 +119,11 @@
     local_grad = lax.dot_general(
         patches, cot_rows, (((0,), (0,)), ((), ())), preferred_element_type=jnp.float32
     )
-    clip_grad = lax.psum(local_grad, "tm")
+    clip_grad = local_grad
+    for hop in (1, 2):
+        clip_grad = clip_grad + lax.ppermute(
+            clip_grad, "tm", [(dev, dev ^ hop) for dev in range(4)]
+        )
     weight_grad = lax.psum_scatter(clip_grad, "dp", scatter_dimension=0, tiled=True)
     return (out_block[None], input_grad[None], weight_grad)
 

time: 399 us -> 536 us (1.34)
  waiting for transfers between devices: 129 us -> 255 us
  other arithmetic: 12.5 us -> 25.2 us
  starting transfers between devices: 3.12 us -> 9.07 us
    ppermute x0 -> x2, waiting for transfers between devices: none -> 164 us  [shards(): lax.ppermute(clip_grad, 'tm', [(dev, dev ^ hop) for dev in range(4)])]
    psum x1 -> x0, waiting for transfers between devices: 35.1 us -> none  [shards(): clip_grad = lax.psum(local_grad, 'tm')]
    add x0 -> x2, other arithmetic: none -> 12.7 us  [shards(): clip_grad + lax.ppermute(clip_grad, 'tm', [(dev, dev ^ hop) for dev in ra...]
    ppermute x0 -> x2, starting transfers between devices: none -> 5.99 us  [shards(): lax.ppermute(clip_grad, 'tm', [(dev, dev ^ hop) for dev in range(4)])]
    unnamed x51 -> x46, local copies, waits for them, and re-layouts: 15.1 us -> 13.6 us
  transfers between devices with their start and end apart: 5 -> 6, of which waited for: 3 -> 4; matrix products, arithmetic and copies ran while one was open for 57% -> 7% of each run, Pallas kernels for 0% -> 0%
where the time goes in v1:
time: 536 us; the launch traced here: 535 us
  waiting for transfers between devices  255 us (48%)
  local copies, waits for them, and re-layouts  204 us (38%)
  other arithmetic  25.2 us (5%)
  blocking collectives  18.1 us (3%)
  between operations  15.3 us (3%)
  starting transfers between devices  9.07 us (2%)
  matrix products  8.11 us (2%)
    slice x27, local copies, waits for them, and re-layouts, unfold(): padded[step_t:step_t + 2 * frames_out:2, step_r:step_r + 2 * rows_out:2,...  176 us
    ppermute x2, waiting for transfers between devices, shards(): lax.ppermute(clip_grad, 'tm', [(dev, dev ^ hop) for dev in range(4)])  164 us
    reduce_scatter x1, waiting for transfers between devices, shards(): lax.psum_scatter(clip_grad, 'dp', scatter_dimension=0, tiled=True)  90.6 us
    unnamed x46, local copies, waits for them, and re-layouts  13.6 us
    add x2, other arithmetic, shards(): clip_grad + lax.ppermute(clip_grad, 'tm', [(dev, dev ^ hop) for dev in ra...  12.7 us
  transfers between devices with their start and end apart: 6, of which 4 were waited for; matrix products, arithmetic and copies ran while one was open for 7% of the time, Pallas kernels for 0%

profile of v1, /device:TPU:0, one launch (start us, length us, event | category | flops | bytes accessed | tf_op | source)
XLA Modules:
  0.0 535.4 jit_solution(13937076589340626032)
XLA Ops:
  10.2 8.4 %all-reduce.11 = (f32[32]{0:T(128)S(1)}, f32[32]{0:T(128)S(1)}) all-reduce(f32[32]{0:T(128)S(1)} %reduce_sum.51, f32[32]{0:T(128)S(1)} %reduce_sum.54), channel_id=1, replica_groups=mesh['dp'=8,'tm'=4] {'tm'}, use_global_device_ids=true, to_apply=%region_2.0 | all-reduce | flops 64 | bytes 512 | tf_op jit(solution)/shard_map/psum | solution.py:76
  18.9 2.0 fusion.15
  24.4 9.8 %slice.130 = bf16[4,8,8,256]{3,2,1,0:T(8,128)(2,1)} slice(bf16[10,17,17,256]{3,2,1,0:T(8,128)(2,1)S(1)} %fusion.38), slice={[0:8:2], [0:16:2], [0:16:2], [0:256:1]} | slice | bytes 262144 | tf_op jit(solution)/shard_map/slice | solution.py:21
  34.2 9.7 %slice.131 = bf16[4,8,8,256]{3,2,1,0:T(8,128)(2,1)} slice(bf16[10,17,17,256]{3,2,1,0:T(8,128)(2,1)S(1)} %fusion.38), slice={[0:8:2], [0:16:2], [1:17:2], [0:256:1]} | slice | bytes 262144 | tf_op jit(solution)/shard_map/slice | solution.py:21
  44.0 9.8 %slice.132 = bf16[4,8,8,256]{3,2,1,0:T(8,128)(2,1)} slice(bf16[10,17,17,256]{3,2,1,0:T(8,128)(2,1)S(1)} %fusion.38), slice={[0:8:2], [0:16:2], [2:17:2], [0:256:1]} | slice | bytes 262144 | tf_op jit(solution)/shard_map/slice | solution.py:21
  53.7 9.7 %slice.133 = bf16[4,8,8,256]{3,2,1,0:T(8,128)(2,1)} slice(bf16[10,17,17,256]{3,2,1,0:T(8,128)(2,1)S(1)} %fusion.38), slice={[0:8:2], [1:17:2], [0:16:2], [0:256:1]} | slice | bytes 262144 | tf_op jit(solution)/shard_map/slice | solution.py:21
  63.5 9.7 %slice.134 = bf16[4,8,8,256]{3,2,1,0:T(8,128)(2,1)} slice(bf16[10,17,17,256]{3,2,1,0:T(8,128)(2,1)S(1)} %fusion.38), slice={[0:8:2], [1:17:2], [1:17:2], [0:256:1]} | slice | bytes 262144 | tf_op jit(solution)/shard_map/slice | solution.py:21
  73.2 9.8 %slice.135 = bf16[4,8,8,256]{3,2,1,0:T(8,128)(2,1)} slice(bf16[10,17,17,256]{3,2,1,0:T(8,128)(2,1)S(1)} %fusion.38), slice={[0:8:2], [1:17:2], [2:17:2], [0:256:1]} | slice | bytes 262144 | tf_op jit(solution)/shard_map/slice | solution.py:21
  82.9 9.7 %slice.136 = bf16[4,8,8,256]{3,2,1,0:T(8,128)(2,1)} slice(bf16[10,17,17,256]{3,2,1,0:T(8,128)(2,1)S(1)} %fusion.38), slice={[0:8:2], [2:17:2], [0:16:2], [0:256:1]} | slice | bytes 262144 | tf_op jit(solution)/shard_map/slice | solution.py:21
  92.6 9.7 %slice.137 = bf16[4,8,8,256]{3,2,1,0:T(8,128)(2,1)} slice(bf16[10,17,17,256]{3,2,1,0:T(8,128)(2,1)S(1)} %fusion.38), slice={[0:8:2], [2:17:2], [1:17:2], [0:256:1]} | slice | bytes 262144 | tf_op jit(solution)/shard_map/slice | solution.py:21
  102.4 9.7 %slice.138 = bf16[4,8,8,256]{3,2,1,0:T(8,128)(2,1)} slice(bf16[10,17,17,256]{3,2,1,0:T(8,128)(2,1)S(1)} %fusion.38), slice={[0:8:2], [2:17:2], [2:17:2], [0:256:1]} | slice | bytes 262144 | tf_op jit(solution)/shard_map/slice | solution.py:21
  112.1 9.7 %slice.139 = bf16[4,8,8,256]{3,2,1,0:T(8,128)(2,1)} slice(bf16[10,17,17,256]{3,2,1,0:T(8,128)(2,1)S(1)} %fusion.38), slice={[1:9:2], [0:16:2], [0:16:2], [0:256:1]} | slice | bytes 262144 | tf_op jit(solution)/shard_map/slice | solution.py:21
  121.8 9.7 %slice.140 = bf16[4,8,8,256]{3,2,1,0:T(8,128)(2,1)} slice(bf16[10,17,17,256]{3,2,1,0:T(8,128)(2,1)S(1)} %fusion.38), slice={[1:9:2], [0:16:2], [1:17:2], [0:256:1]} | slice | bytes 262144 | tf_op jit(solution)/shard_map/slice | solution.py:21
  131.5 9.7 %slice.141 = bf16[4,8,8,256]{3,2,1,0:T(8,128)(2,1)} slice(bf16[10,17,17,256]{3,2,1,0:T(8,128)(2,1)S(1)} %fusion.38), slice={[1:9:2], [0:16:2], [2:17:2], [0:256:1]} | slice | bytes 262144 | tf_op jit(solution)/shard_map/slice | solution.py:21
  141.3 9.7 %slice.142 = bf16[4,8,8,256]{3,2,1,0:T(8,128)(2,1)} slice(bf16[10,17,17,256]{3,2,1,0:T(8,128)(2,1)S(1)} %fusion.38), slice={[1:9:2], [1:17:2], [0:16:2], [0:256:1]} | slice | bytes 262144 | tf_op jit(solution)/shard_map/slice | solution.py:21
  151.0 9.7 %slice.143 = bf16[4,8,8,256]{3,2,1,0:T(8,128)(2,1)} slice(bf16[10,17,17,256]{3,2,1,0:T(8,128)(2,1)S(1)} %fusion.38), slice={[1:9:2], [1:17:2], [1:17:2], [0:256:1]} | slice | bytes 262144 | tf_op jit(solution)/shard_map/slice | solution.py:21
  160.7 9.8 %slice.144 = bf16[4,8,8,256]{3,2,1,0:T(8,128)(2,1)} slice(bf16[10,17,17,256]{3,2,1,0:T(8,128)(2,1)S(1)} %fusion.38), slice={[1:9:2], [1:17:2], [2:17:2], [0:256:1]} | slice | bytes 262144 | tf_op jit(solution)/shard_map/slice | solution.py:21
  170.5 9.7 %slice.145 = bf16[4,8,8,256]{3,2,1,0:T(8,128)(2,1)} slice(bf16[10,17,17,256]{3,2,1,0:T(8,128)(2,1)S(1)} %fusion.38), slice={[1:9:2], [2:17:2], [0:16:2], [0:256:1]} | slice | bytes 262144 | tf_op jit(solution)/shard_map/slice | solution.py:21
  180.2 9.7 %slice.146 = bf16[4,8,8,256]{3,2,1,0:T(8,128)(2,1)} slice(bf16[10,17,17,256]{3,2,1,0:T(8,128)(2,1)S(1)} %fusion.38), slice={[1:9:2], [2:17:2], [1:17:2], [0:256:1]} | slice | bytes 262144 | tf_op jit(solution)/shard_map/slice | solution.py:21
  215.2 3.2 collective-permute-start.2
  218.5 10.9 %collective-permute-done.2 = f32[6912,256]{1,0:T(8,128)S(1)} collective-permute-done((f32[6912,256]{1,0:T(8,128)S(1)}, f32[6912,256]{1,0:T(8,128)S(1)}, u32[]{:S(2)}, u32[]{:S(2)}) %collective-permute-start.2) | collective-permute-done | bytes 7077920 | tf_op jit(solution)/shard_map/ppermute | solution.py:124
  229.4 3.8 add.118
  233.2 2.7 collective-permute-start.3
  236.2 152.7 %collective-permute-done.3 = f32[6912,256]{1,0:T(8,128)} collective-permute-done((f32[6912,256]{1,0:T(8,128)}, f32[6912,256]{1,0:T(8,128)}, u32[]{:S(2)}, u32[]{:S(2)}) %collective-permute-start.3) | collective-permute-done | bytes 7077920 | tf_op jit(solution)/shard_map/ppermute | solution.py:124
  388.9 8.9 %add.119 = f32[6912,256]{1,0:T(8,128)} add(f32[6912,256]{1,0:T(8,128)} %add.118, f32[6912,256]{1,0:T(8,128)} %collective-permute-done.3) | non-fusion elementwise | flops 1769472 | bytes 21233664 | tf_op jit(solution)/shard_map/add | solution.py:124
  398.2 3.1 convolution_bitcast_fusion
  408.0 3.1 copy.39
  411.1 3.5 reshape.271
  417.5 1.9 slice_bitcast_fusion.7
  419.4 3.8 convolution_convert_fusion
  426.3 9.8 %all-reduce.10 = (f32[32]{0:T(128)S(1)}, f32[32]{0:T(128)S(1)}) all-reduce(f32[32]{0:T(128)S(1)} %reduce_sum.75, f32[32]{0:T(128)S(1)} %reduce_sum.72), channel_id=1, replica_groups=mesh['dp'=8,'tm'=4] {'tm'}, use_global_device_ids=true, to_apply=%region_11.12 | all-reduce | flops 64 | bytes 512 | tf_op jit(solution)/shard_map/psum | solution.py:107
  438.0 90.6 %reduce-scatter.2.cloned.1.call-done = f32[864,256]{1,0:T(8,128)} async-done(((f32[6912,256]{1,0:T(8,128)}), f32[864,256]{1,0:T(8,128)}) %reduce-scatter.2.cloned.1.call-update) | async-done | bytes 884752 | tf_op jit(solution)/shard_map/reduce_scatter | solution.py:127
  (110 shorter events, 46.1 us)
Async XLA Ops:
  7.2 206.3 %copy-start = (bf16[1,4,8,8,256]{4,3,2,1,0:T(8,128)(2,1)S(1)}, bf16[1,4,8,8,256]{4,3,2,1,0:T(8,128)(2,1)}, u32[]{:S(2)}) copy-start(bf16[1,4,8,8,256]{4,3,2,1,0:T(8,128)(2,1)} %param.11) | copy-start | bytes 393220
  7.2 391.0 %all-gather.2.cloned.1.call-start = ((), (), s32[]{:S(2)}) async-start(), calls=%async_computation.1 | async-start | bytes 3981312 | tf_op jit(solution)/shard_map/all_gather | solution.py:95
  21.0 2.4 collective-permute-start
  200.3 12.9 %copy-start.7 = (bf16[4,8,8,256]{3,2,1,0:T(8,128)(2,1)S(1)}, bf16[4,8,8,256]{3,2,1,0:T(8,128)(2,1)}, u32[]{:S(2)}) copy-start(bf16[4,8,8,256]{3,2,1,0:T(8,128)(2,1)} %slice.144) | copy-start | bytes 393220
  200.3 13.0 %copy-start.6 = (bf16[4,8,8,256]{3,2,1,0:T(8,128)(2,1)S(1)}, bf16[4,8,8,256]{3,2,1,0:T(8,128)(2,1)}, u32[]{:S(2)}) copy-start(bf16[4,8,8,256]{3,2,1,0:T(8,128)(2,1)} %slice.145) | copy-start | bytes 393220
  200.3 13.0 %copy-start.5 = (bf16[4,8,8,256]{3,2,1,0:T(8,128)(2,1)S(1)}, bf16[4,8,8,256]{3,2,1,0:T(8,128)(2,1)}, u32[]{:S(2)}) copy-start(bf16[4,8,8,256]{3,2,1,0:T(8,128)(2,1)} %slice.146) | copy-start | bytes 393220
  213.5 1.7 copy-start.3
  215.2 14.2 %collective-permute-start.2 = (f32[6912,256]{1,0:T(8,128)S(1)}, f32[6912,256]{1,0:T(8,128)S(1)}, u32[]{:S(2)}, u32[]{:S(2)}) collective-permute-start(f32[6912,256]{1,0:T(8,128)S(1)} %fusion.43), channel_id=1, source_target_pairs={{0,1},{1,0},{2,3},{3,2},{4,5},{5,4},{6,7},{7,6},{8,9},{9,8},{10,11... | collective-permute-start | bytes 21233672 | tf_op jit(solution)/shard_map/ppermute | solution.py:124
  233.2 155.7 %collective-permute-start.3 = (f32[6912,256]{1,0:T(8,128)}, f32[6912,256]{1,0:T(8,128)}, u32[]{:S(2)}, u32[]{:S(2)}) collective-permute-start(f32[6912,256]{1,0:T(8,128)} %add.118), channel_id=1, source_target_pairs={{0,2},{1,3},{2,0},{3,1},{4,6},{5,7},{6,4},{7,5},{8,10},{9,11},{10,... | collective-permute-start | bytes 21233672 | tf_op jit(solution)/shard_map/ppermute | solution.py:124
  236.0 292.6 %reduce-scatter.2.cloned.1.call-start = ((), (), s32[]{:S(2)}) async-start(), calls=%async_computation.2 | async-start | bytes 7962624 | tf_op jit(solution)/shard_map/reduce_scatter | solution.py:127
  414.6 4.8 copy-start.4
  415.9 7.3 %collective-permute-start.1 = (f32[2,16,16,256]{3,2,1,0:T(8,128)S(1)}, f32[2,16,16,256]{3,2,1,0:T(8,128)S(1)}, u32[]{:S(2)}, u32[]{:S(2)}) collective-permute-start(f32[2,16,16,256]{3,2,1,0:T(8,128)S(1)} %slice.183), channel_id=1, source_target_pairs={{1,0},{2,1},{3,2},{5,4},{6,5},{7,6},{9,8},{10,9},{11,10},{13,12},{... | collective-permute-start | bytes 1572872 | tf_op jit(solution)/shard_map/ppermute | solution.py:13
  419.4 5.2 copy-start.2
  419.4 5.2 copy-start.8
  419.4 5.2 copy-start.9
  423.3 105.3 %copy-start.1 = (bf16[1,4,8,8,256]{4,3,2,1,0:T(8,128)(2,1)S(1)}, bf16[1,4,8,8,256]{4,3,2,1,0:T(8,128)(2,1)}, u32[]{:S(2)}) copy-start(bf16[1,4,8,8,256]{4,3,2,1,0:T(8,128)(2,1)} %param.11) | copy-start | bytes 393220
Sparse Core Ops, SparseCore 0:
  236.1 65.5 all-gather.1
  398.0 130.5 reduce-scatter.1
